TPU v7x, 32 devices: a whole 2x2x4 slice. The times are simulated.
32 devices in a mesh: expert: 8 (over z, x), dp: 4 (over y, core).
Axes of the slice: x: 2, y: 2, z: 4, core: 2. Of those that a mesh axis runs over, the one named last changes fastest.
Arguments:
- tokens: bfloat16 [1024, 7168], P('expert'), may hold values from -6 to 6
- routes: int32 [1024, 2], P('expert'), may hold values from 0 to 7, all different within a row; in each aligned block of 128 rows (0 to 127, 128 to 255, ...) at most 96 rows name the same one
- route_gates: bfloat16 [1024, 2], P('expert'), may hold values from 0.049804688 to 1
- cotangent: bfloat16 [1024, 7168], P('expert'), may hold values from -6 to 6
- weight_gate: bfloat16 [8, 7168, 1024], P('expert', None, 'dp'), may hold values from -0.0625 to 0.0625
- weight_up: bfloat16 [8, 7168, 1024], P('expert', None, 'dp'), may hold values from -0.0625 to 0.0625
- weight_down: bfloat16 [8, 1024, 7168], P('expert', 'dp'), may hold values from -0.1875 to 0.1875
Outputs:
- grad_tokens: bfloat16 [1024, 7168], P('expert', 'dp')
- grad_gate: bfloat16 [8, 7168, 1024], P('expert', None, 'dp')
- grad_up: bfloat16 [8, 7168, 1024], P('expert', None, 'dp')
- grad_down: bfloat16 [8, 1024, 7168], P('expert', 'dp')
Inputs may be any that keep to these rules, and one draw needn't show every extreme that they name: `routes`: within each aligned block of 128 rows (the tokens of one index of the expert axis) every row names 2 different experts and no expert is named by more than 96 rows; in every draw some block names some expert exactly 96 times.
All inputs are finite; a program needn't handle non-finite values.
Results may differ from a plain program's by a relative error of at most 0.011.
Values may be sent and summed in bfloat16 or wider, within the bound.
A program may use at most 192 MiB of HBM per device.

v0:
```python
import jax
import jax.numpy as jnp
from jax import lax
from jax.sharding import PartitionSpec as P


def slot_layout(routes, experts, capacity):
    flat_routes = routes.reshape(-1)
    onehot = (flat_routes[:, None] == jnp.arange(experts, dtype=jnp.int32)[None, :]).astype(
        jnp.int32
    )
    before = jnp.cumsum(onehot, axis=0) - onehot
    position = jnp.sum(before * onehot, axis=1)
    slot_index = flat_routes * capacity + position
    total_slots = flat_routes.shape[0]
    owners = (
        jnp.full((experts * capacity,), total_slots, dtype=jnp.int32)
        .at[slot_index]
        .set(jnp.arange(total_slots, dtype=jnp.int32))
    )
    return (slot_index, owners)


def pad_rows(source_array, owners, top_count):
    extended = jnp.concatenate(
        [source_array, jnp.zeros((1,) + source_array.shape[1:], source_array.dtype)], 0
    )
    return extended[owners // top_count]


def per_device(tokens, routes, route_gates, cotangent, weight_gate, weight_up, weight_down):
    members = lax.axis_size("expert")
    groups = lax.axis_size("dp")
    local_experts = weight_gate.shape[0]
    experts = members * local_experts
    token_rows = routes.shape[0]
    top_count = routes.shape[1]
    width = tokens.shape[1]
    quarter = width // groups
    capacity = 3 * token_rows * top_count // experts
    slot_index, owners = slot_layout(routes, experts, capacity)
    gate_flat = jnp.concatenate([route_gates.reshape(-1), jnp.zeros((1,), route_gates.dtype)], 0)
    gate_send = gate_flat[owners].reshape(experts, capacity)
    token_send = pad_rows(tokens, owners, top_count).reshape(experts, capacity, width)
    back_send = pad_rows(cotangent, owners, top_count).reshape(experts, capacity, width)
    token_arrived, back_arrived, gate_arrived = (
        lax.all_to_all(token_send, "expert", split_axis=0, concat_axis=1, tiled=True),
        lax.all_to_all(back_send, "expert", split_axis=0, concat_axis=1, tiled=True),
        lax.all_to_all(gate_send, "expert", split_axis=0, concat_axis=1, tiled=True),
    )
    scale = gate_arrived.astype(jnp.float32)[:, :, None]
    pre_gate = jnp.einsum(
        "erd,edf->erf", token_arrived, weight_gate, preferred_element_type=jnp.float32
    )
    pre_up = jnp.einsum(
        "erd,edf->erf", token_arrived, weight_up, preferred_element_type=jnp.float32
    )
    sigma = jax.nn.sigmoid(pre_gate)
    activated = pre_gate * sigma
    scaled_hidden = (scale * activated * pre_up).astype(jnp.bfloat16)
    back_hidden = scale * jnp.einsum(
        "erd,efd->erf", back_arrived, weight_down, preferred_element_type=jnp.float32
    )
    back_up = (back_hidden * activated).astype(jnp.bfloat16)
    back_gate = (back_hidden * pre_up * sigma * (1.0 + pre_gate * (1.0 - sigma))).astype(
        jnp.bfloat16
    )
    grad_gate = jnp.einsum(
        "erd,erf->edf", token_arrived, back_gate, preferred_element_type=jnp.float32
    ).astype(jnp.bfloat16)
    grad_up = jnp.einsum(
        "erd,erf->edf", token_arrived, back_up, preferred_element_type=jnp.float32
    ).astype(jnp.bfloat16)
    grad_down = jnp.einsum(
        "erf,erd->efd", scaled_hidden, back_arrived, preferred_element_type=jnp.float32
    ).astype(jnp.bfloat16)
    up_term = jnp.einsum("edf,erf->der", weight_up, back_up, preferred_element_type=jnp.float32)
    gate_term = jnp.einsum(
        "edf,erf->der", weight_gate, back_gate, preferred_element_type=jnp.float32
    )
    slot_back = lax.psum_scatter(
        (up_term + gate_term).astype(jnp.bfloat16), "dp", scatter_dimension=0, tiled=True
    )
    returned = lax.all_to_all(slot_back, "expert", split_axis=2, concat_axis=1, tiled=True)
    flat_back = returned.reshape(quarter, experts * capacity)
    picked = (
        jnp.take(flat_back, slot_index, axis=1)
        .astype(jnp.float32)
        .reshape(quarter, token_rows, top_count)
    )
    grad_tokens = jnp.sum(picked, axis=2).T.astype(jnp.bfloat16)
    return (grad_tokens, grad_gate, grad_up, grad_down)


def solution(mesh):
    placed = (
        P("expert", None),
        P("expert", None),
        P("expert", None),
        P("expert", None),
        P("expert", None, "dp"),
        P("expert", None, "dp"),
        P("expert", "dp", None),
    )
    return jax.shard_map(
        per_device,
        mesh=mesh,
        in_specs=placed,
        out_specs=(
            P("expert", "dp"),
            P("expert", None, "dp"),
            P("expert", None, "dp"),
            P("expert", "dp", None),
        ),
        check_vma=False,
    )
```

profile of v0, /device:TPU:0, one launch (start us, length us, event | category | flops | bytes accessed | tf_op | source)
XLA Modules:
  0.0 770.3 jit_solution(8576594936999472891)
XLA Ops:
  7.2 0.7 broadcast_multiply_fusion
  7.8 0.8 copy.30
  8.6 0.1 eq.26
  8.8 0.1 reshape.180
  8.9 0.8 copy.34
  9.7 0.1 reshape.182
  9.9 0.1 copy.35
  10.0 0.1 mul.69
  10.1 0.6 reduce-window.6
  10.7 0.2 slice_reduce_fusion
  11.0 0.1 fusion.21
  11.1 1.4 scatter_custom_fusion
  12.5 5.0 gather_fusion
  17.5 0.7 all_to_all.16
  18.2 7.3 all-to-all-start
  25.5 1.7 concatenate.11
  27.2 9.4 %gather_fusion.2 = bf16[768,7168]{1,0:T(8,128)(2,1)} fusion(bf16[129,7168]{1,0:T(8,128)(2,1)S(1)} %concatenate.11, s32[1024]{0:T(1024)S(1)} %get-tuple-element.9), kind=kCustom, calls=%fused_computation.2 | custom fusion | bytes 22023168 | tf_op jit(solution)/shard_map/gather | solution.py:28
  36.6 6.0 all-to-all-start.2
  42.6 1.7 concatenate.10
  44.3 9.5 %gather_fusion.1 = bf16[768,7168]{1,0:T(8,128)(2,1)} fusion(bf16[129,7168]{1,0:T(8,128)(2,1)S(1)} %concatenate.10, s32[1024]{0:T(1024)S(1)} %get-tuple-element.9), kind=kCustom, calls=%fused_computation.1 | custom fusion | bytes 22023168 | tf_op jit(solution)/shard_map/gather | solution.py:28
  53.7 227.6 %all-to-all-done.2 = bf16[8,96,7168]{2,1,0:T(8,128)(2,1)} async-done(((bf16[8,96,7168]{2,1,0:T(8,128)(2,1)}), bf16[8,96,7168]{2,1,0:T(8,128)(2,1)}, u32[]{:S(2)}, u32[]{:S(2)}) %all-to-all-start.2) | async-done | bytes 11010080 | tf_op jit(solution)/shard_map/all_to_all | solution.py:47
  281.4 5.2 all-to-all-start.1
  286.6 0.3 reduce-scatter.2.cloned.1.call-start
  287.0 6.9 fusion.4
  293.9 230.6 %all-to-all-done.1 = bf16[8,96,7168]{2,1,0:T(8,128)(2,1)} async-done(((bf16[8,96,7168]{2,1,0:T(8,128)(2,1)}), bf16[8,96,7168]{2,1,0:T(8,128)(2,1)}, u32[]{:S(2)}, u32[]{:S(2)}) %all-to-all-start.1) | async-done | bytes 11010080 | tf_op jit(solution)/shard_map/all_to_all | solution.py:48
  524.5 7.1 fusion.13
  531.6 8.3 %multiply_convert_fusion.1 = (bf16[768,256]{1,0:T(8,128)(2,1)S(1)}, bf16[768,256]{1,0:T(8,128)(2,1)S(1)}, f32[768,256]{1,0:T(8,128)}) fusion(f32[768,256]{1,0:T(8,128)S(1)} %fusion.13, f32[768,256]{1,0:T(8,128)S(1)} %fusion.4, bf16[768,7168]{1,0:T(8,128)(2,1)} %bitcast.8, bf16[1,7168,256]{2,1,0:T(8,128)(2,1)S(1)} %copy-done.1), kind=kOutput, calls=%fused_computation.27 | convolution fusion | flops 2821128192 | bytes 17825792 | tf_op jit(solution)/shard_map/erd,edf->erf/dot_general | solution.py:52
  540.0 9.1 %fusion.6 = f32[768,7168]{1,0:T(8,128)} fusion(bf16[768,256]{1,0:T(8,128)(2,1)S(1)} %get-tuple-element.5, bf16[1,7168,256]{2,1,0:T(8,128)(2,1)S(1)} %copy-done), kind=kOutput, calls=%fused_computation.15 | convolution fusion | flops 2818572288 | bytes 26083328 | tf_op jit(solution)/shard_map/edf,erf->der/dot_general | solution.py:77
  549.0 12.8 %fusion = bf16[7168,1,768]{0,2,1:T(8,128)(2,1)} fusion(f32[768,7168]{1,0:T(8,128)} %fusion.6, bf16[768,256]{1,0:T(8,128)(2,1)S(1)} %get-tuple-element.4, bf16[1,7168,256]{2,1,0:T(8,128)(2,1)S(1)} %copy-done.1), kind=kOutput, calls=%fused_computation.6 | convolution fusion | flops 2829582336 | bytes 37093376 | tf_op jit(solution)/shard_map/edf,erf->der/dot_general | solution.py:78
  561.9 88.4 %reduce-scatter.2.cloned.1.call-done = bf16[1792,1,768]{0,2,1:T(8,128)(2,1)} async-done(((bf16[7168,1,768]{0,2,1:T(8,128)(2,1)}), bf16[1792,1,768]{0,2,1:T(8,128)(2,1)}) %reduce-scatter.2.cloned.1.call-update) | async-done | bytes 2752528 | tf_op jit(solution)/shard_map/reduce_scatter | solution.py:81
  650.3 8.4 %copy.44 = bf16[1792,1,768]{0,1,2:T(2,128)(2,1)} copy(bf16[1792,1,768]{0,2,1:T(8,128)(2,1)} %reduce-scatter.2.cloned.1.call-done) | data formatting | bytes 5505024 | tf_op jit(solution)/shard_map/reduce_scatter | solution.py:81
  658.7 0.5 broadcast.118
  659.2 17.0 %reduce.7 = bf16[768,1792]{1,0:T(8,128)(2,1)S(1)} reduce(bf16[768,1,1792]{2,1,0:T(2,128)(2,1)} %bitcast.67, bf16[]{:T(256)} %broadcast.118), dimensions={1}, to_apply=%bitcast.62.reduce_sub_computation | reduce | bytes 5505026
  676.3 3.5 reshape.245
  679.7 5.7 all-to-all-start.3
  685.4 0.8 reduce_sum.26
  686.2 0.9 copy.32
  687.1 0.5 compare_and_fusion
  687.6 1.4 copy.33
  689.0 9.5 %fusion.3 = bf16[1,256,7168]{2,1,0:T(8,128)(2,1)} fusion(bf16[768,7168]{1,0:T(8,128)(2,1)} %bitcast.5, f32[768,256]{1,0:T(8,128)S(1)} %fusion.4, f32[768]{0:T(1024)S(1)} %reshape.191, f32[768,256]{1,0:T(8,128)} %get-tuple-element.8), kind=kOutput, calls=%fused_computation.12 | convolution fusion | flops 2821783552 | bytes 16256000 | tf_op jit(solution)/shard_map/erf,erd->efd/dot_general | solution.py:74
  698.5 9.1 %fusion.1 = bf16[1,7168,256]{2,1,0:T(8,128)(2,1)} fusion(bf16[768,7168]{1,0:T(8,128)(2,1)} %bitcast.8, bf16[768,256]{1,0:T(8,128)(2,1)S(1)} %copy-done.3), kind=kOutput, calls=%fused_computation.10 | convolution fusion | flops 2820407296 | bytes 15073280 | tf_op jit(solution)/shard_map/erd,erf->edf/dot_general | solution.py:68
  707.6 9.1 %fusion.2 = bf16[1,7168,256]{2,1,0:T(8,128)(2,1)} fusion(bf16[768,7168]{1,0:T(8,128)(2,1)} %bitcast.8, bf16[768,256]{1,0:T(8,128)(2,1)S(1)} %copy-done.5), kind=kOutput, calls=%fused_computation.11 | convolution fusion | flops 2820407296 | bytes 15073280 | tf_op jit(solution)/shard_map/erd,erf->edf/dot_general | solution.py:71
  716.7 31.0 %all-to-all-done.3 = bf16[8,2,86016]{2,1,0:T(2,128)(2,1)S(1)} async-done(((bf16[8,2,86016]{2,1,0:T(2,128)(2,1)}), bf16[8,2,86016]{2,1,0:T(2,128)(2,1)S(1)}, u32[]{:S(2)}, u32[]{:S(2)}) %all-to-all-start.3) | async-done | bytes 2752544 | tf_op jit(solution)/shard_map/all_to_all | solution.py:84
  747.7 4.9 reshape.246
  752.6 3.0 copy.43
  755.6 2.3 gather_fusion.3
  757.9 2.5 gather.19
  760.4 2.8 fusion.16
  (29 shorter events, 0.2 us)
Async XLA Ops:
  18.2 18.3 %all-to-all-start = ((bf16[8,1,96]{2,1,0:T(2,128)(2,1)}), bf16[8,1,96]{2,1,0:T(2,128)(2,1)S(1)}, u32[]{:S(2)}, u32[]{:S(2)}) async-start(bf16[8,1,96]{2,1,0:T(2,128)(2,1)} %all_to_all.16), calls=%async_computation | async-start | bytes 8192 | tf_op jit(solution)/shard_map/all_to_all | solution.py:49
  36.6 244.8 %all-to-all-start.2 = ((bf16[8,96,7168]{2,1,0:T(8,128)(2,1)}), bf16[8,96,7168]{2,1,0:T(8,128)(2,1)}, u32[]{:S(2)}, u32[]{:S(2)}) async-start(bf16[8,96,7168]{2,1,0:T(8,128)(2,1)} %bitcast.65), calls=%async_computation.2 | async-start | bytes 22020096 | tf_op jit(solution)/shard_map/all_to_all | solution.py:47
  281.4 243.2 %all-to-all-start.1 = ((bf16[8,96,7168]{2,1,0:T(8,128)(2,1)}), bf16[8,96,7168]{2,1,0:T(8,128)(2,1)}, u32[]{:S(2)}, u32[]{:S(2)}) async-start(bf16[8,96,7168]{2,1,0:T(8,128)(2,1)} %bitcast.64), calls=%async_computation.1 | async-start | bytes 22020096 | tf_op jit(solution)/shard_map/all_to_all | solution.py:48
  286.6 363.7 %reduce-scatter.2.cloned.1.call-start = ((), (), s32[]{:S(2)}) async-start(), calls=%async_computation.5 | async-start | bytes 13762560 | tf_op jit(solution)/shard_map/reduce_scatter | solution.py:81
  524.5 7.1 copy-start.1
  531.6 8.3 %copy-start = (bf16[1,7168,256]{2,1,0:T(8,128)(2,1)S(1)}, bf16[1,7168,256]{2,1,0:T(8,128)(2,1)}, u32[]{:S(2)}) copy-start(bf16[1,7168,256]{2,1,0:T(8,128)(2,1)} %param.12) | copy-start | bytes 11010052
  540.0 9.1 %copy-start.4 = (bf16[768,256]{1,0:T(8,128)(2,1)}, bf16[768,256]{1,0:T(8,128)(2,1)S(1)}, u32[]{:S(2)}) copy-start(bf16[768,256]{1,0:T(8,128)(2,1)S(1)} %get-tuple-element.5) | copy-start | bytes 1179652
  540.0 9.1 %copy-start.2 = (bf16[768,256]{1,0:T(8,128)(2,1)}, bf16[768,256]{1,0:T(8,128)(2,1)S(1)}, u32[]{:S(2)}) copy-start(bf16[768,256]{1,0:T(8,128)(2,1)S(1)} %get-tuple-element.4) | copy-start | bytes 1179652
  676.2 10.9 %copy-start.7 = (s32[128,2]{0,1:T(2,128)S(1)}, s32[128,2]{0,1:T(2,128)}, u32[]{:S(2)}) copy-start(s32[128,2]{0,1:T(2,128)} %param.8) | copy-start | bytes 3076
  679.7 68.0 %all-to-all-start.3 = ((bf16[8,2,86016]{2,1,0:T(2,128)(2,1)}), bf16[8,2,86016]{2,1,0:T(2,128)(2,1)S(1)}, u32[]{:S(2)}, u32[]{:S(2)}) async-start(bf16[8,2,86016]{2,1,0:T(2,128)(2,1)} %reshape.245), calls=%async_computation.4 | async-start | bytes 5505024 | tf_op jit(solution)/shard_map/all_to_all | solution.py:84
  689.0 9.5 %copy-start.3 = (bf16[768,256]{1,0:T(8,128)(2,1)S(1)}, bf16[768,256]{1,0:T(8,128)(2,1)}, u32[]{:S(2)}) copy-start(bf16[768,256]{1,0:T(8,128)(2,1)} %copy-done.2) | copy-start | bytes 1179652
  698.5 9.1 %copy-start.5 = (bf16[768,256]{1,0:T(8,128)(2,1)S(1)}, bf16[768,256]{1,0:T(8,128)(2,1)}, u32[]{:S(2)}) copy-start(bf16[768,256]{1,0:T(8,128)(2,1)} %copy-done.4) | copy-start | bytes 1179652
  752.6 7.8 %copy-start.6 = (pred[128,2]{1,0:T(8,128)(4,1)S(1)}, pred[128,2]{1,0:T(8,128)(4,1)}, u32[]{:S(2)}) copy-start(pred[128,2]{1,0:T(8,128)(4,1)} %copy.33) | copy-start | bytes 772
Sparse Core Ops, SparseCore 0:
  562.0 88.2 reduce-scatter.1
where the time goes:
time: 776 us; the launch traced here: 770 us
  waiting for transfers between devices  578 us (74%)
  matrix products  71.9 us (9%)
  local copies, waits for them, and re-layouts  60 us (8%)
  starting transfers between devices  24.5 us (3%)
  other arithmetic  21.8 us (3%)
  between operations  14.5 us (2%)
    all_to_all x1, waiting for transfers between devices, per_device(): lax.all_to_all(back_send, 'expert', split_axis=0, concat_axis=1, tiled=True)  231 us
    all_to_all x1, waiting for transfers between devices, per_device(): lax.all_to_all(token_send, 'expert', split_axis=0, concat_axis=1, tiled=T...  228 us
    reduce_scatter x1, waiting for transfers between devices, per_device(): lax.psum_scatter((up_term + gate_term).astype(jnp.bfloat16), 'dp', scatte...  88.4 us
    all_to_all x1, waiting for transfers between devices, per_device(): lax.all_to_all(slot_back, 'expert', split_axis=2, concat_axis=1, tiled=True)  31 us
    gather x2, local copies, waits for them, and re-layouts, pad_rows(): return extended[owners // top_count]  18.9 us
    unnamed x1, other arithmetic  17 us
  transfers between devices with their start and end apart: 5, of which 4 were waited for; matrix products, arithmetic and copies ran while one was open for 8% of the time, Pallas kernels for 0%

commit v1 on v0

--- a/solution.py
+++ b/solution.py
@@ -2,6 +2,7 @@
 import jax.numpy as jnp
 from jax import lax
 from jax.sharding import PartitionSpec as P
+from jax.lax import axis_index, axis_size, ppermute
 
 
 def slot_layout(routes, experts, capacity):
@@ -81,7 +82,23 @@
     slot_back = lax.psum_scatter(
         (up_term + gate_term).astype(jnp.bfloat16), "dp", scatter_dimension=0, tiled=True
     )
-    returned = lax.all_to_all(slot_back, "expert", split_axis=2, concat_axis=1, tiled=True)
+    everything = axis_size("expert")
+    response, new = (everything, axis_index("expert"))
+    b_next = slot_back.shape[2] // response
+    e_now = list(slot_back.shape)
+    e_now[2] = b_next
+    piece_out = e_now[1]
+    e_now[1] = piece_out * response
+    returned = jnp.zeros(e_now, slot_back.dtype)
+    for k0 in [*range(response)]:
+        work_now = lax.dynamic_slice_in_dim(slot_back, (new ^ k0) * b_next, b_next, axis=2)
+        if k0:
+            work_now = ppermute(
+                work_now, axis_name="expert", perm=[(tick, tick ^ k0) for tick in range(response)]
+            )
+        returned = lax.dynamic_update_slice_in_dim(
+            returned, work_now, (new ^ k0) * piece_out, axis=1
+        )
     flat_back = returned.reshape(quarter, experts * capacity)
     picked = (
         jnp.take(flat_back, slot_index, axis=1)

time: 776 us -> 745 us (0.960)
  local copies, waits for them, and re-layouts: 60 us -> 39.9 us
  other arithmetic: 21.8 us -> 4.29 us
    ppermute x0 -> x7, waiting for transfers between devices: none -> 58.3 us  [per_device(): ppermute(work_now, axis_name='expert', perm=[(tick, tick ^ k0) for tick i...]
    all_to_all x1 -> x0, waiting for transfers between devices: 31 us -> none  [per_device(): lax.all_to_all(slot_back, 'expert', split_axis=2, concat_axis=1, tiled=True)]
    reduce_scatter x1, waiting for transfers between devices: 88.4 us -> 65.7 us  [per_device(): lax.psum_scatter((up_term + gate_term).astype(jnp.bfloat16), 'dp', scatte...]
    unnamed x1 -> x0, other arithmetic: 17 us -> none
    ppermute x0 -> x7, starting transfers between devices: none -> 10.8 us  [per_device(): ppermute(work_now, axis_name='expert', perm=[(tick, tick ^ k0) for tick i...]
    reduce_scatter x1 -> x0, local copies, waits for them, and re-layouts: 8.41 us -> none  [per_device(): lax.psum_scatter((up_term + gate_term).astype(jnp.bfloat16), 'dp', scatte...]
  transfers between devices with their start and end apart: 5 -> 11, of which waited for: 4 -> 5; matrix products, arithmetic and copies ran while one was open for 8% -> 8% of each run, Pallas kernels for 0% -> 0%
where the time goes in v1:
time: 745 us; the launch traced here: 744 us
  waiting for transfers between devices  582 us (78%)
  matrix products  73.9 us (10%)
  local copies, waits for them, and re-layouts  39.9 us (5%)
  starting transfers between devices  29.5 us (4%)
  between operations  14.4 us (2%)
    all_to_all x1, waiting for transfers between devices, per_device(): lax.all_to_all(back_send, 'expert', split_axis=0, concat_axis=1, tiled=True)  231 us
    all_to_all x1, waiting for transfers between devices, per_device(): lax.all_to_all(token_send, 'expert', split_axis=0, concat_axis=1, tiled=T...  228 us
    reduce_scatter x1, waiting for transfers between devices, per_device(): lax.psum_scatter((up_term + gate_term).astype(jnp.bfloat16), 'dp', scatte...  65.7 us
    ppermute x7, waiting for transfers between devices, per_device(): ppermute(work_now, axis_name='expert', perm=[(tick, tick ^ k0) for tick i...  58.3 us
    gather x2, local copies, waits for them, and re-layouts, pad_rows(): return extended[owners // top_count]  18.8 us
  transfers between devices with their start and end apart: 11, of which 5 were waited for; matrix products, arithmetic and copies ran while one was open for 8% of the time, Pallas kernels for 0%

profile of v1, /device:TPU:0, one launch (start us, length us, event | category | flops | bytes accessed | tf_op | source)
XLA Modules:
  0.0 744.4 jit_solution(1938303001867056463)
XLA Ops:
  7.2 0.7 broadcast_multiply_fusion
  7.8 0.8 copy.21
  8.6 0.1 eq.26
  8.8 0.1 reshape.176
  8.9 0.8 copy.25
  9.7 0.1 reshape.178
  10.0 0.1 mul.93
  10.1 0.6 reduce-window.6
  10.7 0.2 slice_reduce_fusion
  11.1 1.4 scatter_custom_fusion
  12.5 5.0 gather_fusion
  17.5 0.7 all_to_all.13
  18.2 7.3 all-to-all-start
  25.5 1.7 concatenate.11
  27.2 9.4 %gather_fusion.2 = bf16[768,7168]{1,0:T(8,128)(2,1)} fusion(bf16[129,7168]{1,0:T(8,128)(2,1)S(1)} %concatenate.11, s32[1024]{0:T(1024)S(1)} %get-tuple-element.17), kind=kCustom, calls=%fused_computation.2 | custom fusion | bytes 22023168 | tf_op jit(solution)/shard_map/gather | solution.py:29
  36.5 6.0 all-to-all-start.2
  42.5 1.7 concatenate.10
  44.2 9.5 %gather_fusion.1 = bf16[768,7168]{1,0:T(8,128)(2,1)} fusion(bf16[129,7168]{1,0:T(8,128)(2,1)S(1)} %concatenate.10, s32[1024]{0:T(1024)S(1)} %get-tuple-element.17), kind=kCustom, calls=%fused_computation.1 | custom fusion | bytes 22023168 | tf_op jit(solution)/shard_map/gather | solution.py:29
  53.7 227.6 %all-to-all-done.2 = bf16[8,96,7168]{2,1,0:T(8,128)(2,1)} async-done(((bf16[8,96,7168]{2,1,0:T(8,128)(2,1)}), bf16[8,96,7168]{2,1,0:T(8,128)(2,1)}, u32[]{:S(2)}, u32[]{:S(2)}) %all-to-all-start.2) | async-done | bytes 11010080 | tf_op jit(solution)/shard_map/all_to_all | solution.py:48
  281.3 5.2 all-to-all-start.1
  286.6 0.2 reduce-scatter.2.cloned.1.call-start
  286.9 6.9 fusion.4
  293.8 230.7 %all-to-all-done.1 = bf16[8,96,7168]{2,1,0:T(8,128)(2,1)} async-done(((bf16[8,96,7168]{2,1,0:T(8,128)(2,1)}), bf16[8,96,7168]{2,1,0:T(8,128)(2,1)}, u32[]{:S(2)}, u32[]{:S(2)}) %all-to-all-start.1) | async-done | bytes 11010080 | tf_op jit(solution)/shard_map/all_to_all | solution.py:49
  524.5 7.1 fusion.13
  531.6 8.3 %multiply_convert_fusion.1 = (bf16[768,256]{1,0:T(8,128)(2,1)S(1)}, bf16[768,256]{1,0:T(8,128)(2,1)S(1)}, f32[768,256]{1,0:T(8,128)}) fusion(f32[768,256]{1,0:T(8,128)S(1)} %fusion.13, f32[768,256]{1,0:T(8,128)S(1)} %fusion.4, bf16[768,7168]{1,0:T(8,128)(2,1)} %bitcast.8, bf16[1,7168,256]{2,1,0:T(8,128)(2,1)S(1)} %copy-done.1), kind=kOutput, calls=%fused_computation.26 | convolution fusion | flops 2821128192 | bytes 17825792 | tf_op jit(solution)/shard_map/erd,edf->erf/dot_general | solution.py:53
  539.9 9.1 %fusion.6 = f32[768,7168]{1,0:T(8,128)} fusion(bf16[768,256]{1,0:T(8,128)(2,1)S(1)} %get-tuple-element.13, bf16[1,7168,256]{2,1,0:T(8,128)(2,1)S(1)} %copy-done), kind=kOutput, calls=%fused_computation.15 | convolution fusion | flops 2818572288 | bytes 26083328 | tf_op jit(solution)/shard_map/edf,erf->der/dot_general | solution.py:78
  549.0 12.4 %fusion = bf16[7168,1,768]{0,2,1:T(8,128)(2,1)} fusion(f32[768,7168]{1,0:T(8,128)} %fusion.6, bf16[768,256]{1,0:T(8,128)(2,1)S(1)} %get-tuple-element.12, bf16[1,7168,256]{2,1,0:T(8,128)(2,1)S(1)} %copy-done.1), kind=kOutput, calls=%fused_computation.6 | convolution fusion | flops 2829582336 | bytes 37093376 | tf_op jit(solution)/shard_map/edf,erf->der/dot_general | solution.py:79
  561.5 0.1 reduce_sum.26
  561.7 0.4 copy-done.7
  562.1 0.7 copy.24
  562.8 10.1 %fusion.1 = bf16[1,7168,256]{2,1,0:T(8,128)(2,1)} fusion(bf16[768,7168]{1,0:T(8,128)(2,1)} %bitcast.8, bf16[768,256]{1,0:T(8,128)(2,1)S(1)} %get-tuple-element.12), kind=kOutput, calls=%fused_computation.10 | convolution fusion | flops 2820407296 | bytes 15073280 | tf_op jit(solution)/shard_map/erd,erf->edf/dot_general | solution.py:69
  572.9 11.1 %fusion.2 = bf16[1,7168,256]{2,1,0:T(8,128)(2,1)} fusion(bf16[768,7168]{1,0:T(8,128)(2,1)} %bitcast.8, bf16[768,256]{1,0:T(8,128)(2,1)S(1)} %copy-done.5), kind=kOutput, calls=%fused_computation.11 | convolution fusion | flops 2820407296 | bytes 15073280 | tf_op jit(solution)/shard_map/erd,erf->edf/dot_general | solution.py:72
  584.0 65.7 %reduce-scatter.2.cloned.1.call-done = bf16[1792,1,768]{0,2,1:T(8,128)(2,1)} async-done(((bf16[7168,1,768]{0,2,1:T(8,128)(2,1)}), bf16[1792,1,768]{0,2,1:T(8,128)(2,1)}) %reduce-scatter.2.cloned.1.call-update) | async-done | bytes 2752528 | tf_op jit(solution)/shard_map/reduce_scatter | solution.py:82
  649.7 0.2 broadcast_in_dim.27
  649.9 1.6 copy-done.2
  651.5 0.2 constant_dynamic-slice_fusion
  651.7 1.6 collective-permute-start.1
  653.3 1.5 collective-permute-start
  654.7 9.0 %fusion.3 = bf16[1,256,7168]{2,1,0:T(8,128)(2,1)} fusion(bf16[768,7168]{1,0:T(8,128)(2,1)} %bitcast.5, f32[768,256]{1,0:T(8,128)S(1)} %fusion.4, f32[768]{0:T(1024)S(1)} %reshape.187, f32[768,256]{1,0:T(8,128)S(1)} %copy-done.3), kind=kOutput, calls=%fused_computation.12 | convolution fusion | flops 2821783552 | bytes 16256000 | tf_op jit(solution)/shard_map/erf,erd->efd/dot_general | solution.py:75
  663.7 2.4 collective-permute-start.6
  666.1 1.5 collective-permute-start.5
  667.5 1.5 collective-permute-start.4
  669.0 2.3 collective-permute-start.2
  671.5 29.0 %collective-permute-done.2 = bf16[1792,1,96]{0,2,1:T(8,128)(2,1)S(1)} collective-permute-done((bf16[1792,1,96]{0,2,1:T(8,128)(2,1)S(1)}, bf16[1792,1,96]{0,2,1:T(8,128)(2,1)S(1)}, u32[]{:S(2)}, u32[]{:S(2)}) %collective-permute-start.2) | collective-permute-done | bytes 344096 | tf_op jit(solution)/shard_map/ppermute | solution.py:96
  700.6 29.3 %collective-permute-done.3 = bf16[1792,1,96]{0,2,1:T(8,128)(2,1)S(1)} collective-permute-done((bf16[1792,1,96]{0,2,1:T(8,128)(2,1)S(1)}, bf16[1792,1,96]{0,2,1:T(8,128)(2,1)S(1)}, u32[]{:S(2)}, u32[]{:S(2)}) %collective-permute-start.3) | collective-permute-done | bytes 344096 | tf_op jit(solution)/shard_map/ppermute | solution.py:96
  730.1 2.3 gather_fusion.3
  732.4 2.3 gather.19
  734.7 2.8 fusion.16
  (44 shorter events, 0.8 us)
Async XLA Ops:
  18.2 18.3 %all-to-all-start = ((bf16[8,1,96]{2,1,0:T(2,128)(2,1)}), bf16[8,1,96]{2,1,0:T(2,128)(2,1)S(1)}, u32[]{:S(2)}, u32[]{:S(2)}) async-start(bf16[8,1,96]{2,1,0:T(2,128)(2,1)} %all_to_all.13), calls=%async_computation | async-start | bytes 8192 | tf_op jit(solution)/shard_map/all_to_all | solution.py:50
  36.5 244.8 %all-to-all-start.2 = ((bf16[8,96,7168]{2,1,0:T(8,128)(2,1)}), bf16[8,96,7168]{2,1,0:T(8,128)(2,1)}, u32[]{:S(2)}, u32[]{:S(2)}) async-start(bf16[8,96,7168]{2,1,0:T(8,128)(2,1)} %bitcast.58), calls=%async_computation.2 | async-start | bytes 22020096 | tf_op jit(solution)/shard_map/all_to_all | solution.py:48
  281.3 243.2 %all-to-all-start.1 = ((bf16[8,96,7168]{2,1,0:T(8,128)(2,1)}), bf16[8,96,7168]{2,1,0:T(8,128)(2,1)}, u32[]{:S(2)}, u32[]{:S(2)}) async-start(bf16[8,96,7168]{2,1,0:T(8,128)(2,1)} %bitcast.57), calls=%async_computation.1 | async-start | bytes 22020096 | tf_op jit(solution)/shard_map/all_to_all | solution.py:49
  286.6 363.2 %reduce-scatter.2.cloned.1.call-start = ((), (), s32[]{:S(2)}) async-start(), calls=%async_computation.4 | async-start | bytes 13762560 | tf_op jit(solution)/shard_map/reduce_scatter | solution.py:82
  524.5 7.1 copy-start.1
  531.6 8.3 %copy-start = (bf16[1,7168,256]{2,1,0:T(8,128)(2,1)S(1)}, bf16[1,7168,256]{2,1,0:T(8,128)(2,1)}, u32[]{:S(2)}) copy-start(bf16[1,7168,256]{2,1,0:T(8,128)(2,1)} %param.12) | copy-start | bytes 11010052
  539.9 9.1 %copy-start.4 = (bf16[768,256]{1,0:T(8,128)(2,1)}, bf16[768,256]{1,0:T(8,128)(2,1)S(1)}, u32[]{:S(2)}) copy-start(bf16[768,256]{1,0:T(8,128)(2,1)S(1)} %get-tuple-element.13) | copy-start | bytes 1179652
  561.4 0.7 copy-start.7
  562.8 10.1 %copy-start.5 = (bf16[768,256]{1,0:T(8,128)(2,1)S(1)}, bf16[768,256]{1,0:T(8,128)(2,1)}, u32[]{:S(2)}) copy-start(bf16[768,256]{1,0:T(8,128)(2,1)} %copy-done.4) | copy-start | bytes 1179652
  649.7 1.8 copy-start.2
  649.7 5.0 copy-start.3
  651.7 19.7 %collective-permute-start.1 = (bf16[1792,1,96]{0,2,1:T(8,128)(2,1)S(1)}, bf16[1792,1,96]{0,2,1:T(8,128)(2,1)S(1)}, u32[]{:S(2)}, u32[]{:S(2)}) collective-permute-start(bf16[1792,1,96]{0,2,1:T(8,128)(2,1)S(1)} %get-tuple-element.9), channel_id=1, source_target_pairs={{0,8},{4,12},{8,0},{12,4},{16,24},{20,28},{24,16},{28,20},{1,9},{5... | collective-permute-start | bytes 1032200 | tf_op jit(solution)/shard_map/ppermute | solution.py:96
  653.3 15.8 %collective-permute-start = (bf16[1792,1,96]{0,2,1:T(8,128)(2,1)S(1)}, bf16[1792,1,96]{0,2,1:T(8,128)(2,1)S(1)}, u32[]{:S(2)}, u32[]{:S(2)}) collective-permute-start(bf16[1792,1,96]{0,2,1:T(8,128)(2,1)S(1)} %get-tuple-element.10), channel_id=1, source_target_pairs={{0,4},{4,0},{8,12},{12,8},{16,20},{20,16},{24,28},{28,24},{1,5},{5... | collective-permute-start | bytes 1032200 | tf_op jit(solution)/shard_map/ppermute | solution.py:96
  663.7 66.3 %collective-permute-start.6 = (bf16[1792,1,96]{0,2,1:T(8,128)(2,1)S(1)}, bf16[1792,1,96]{0,2,1:T(8,128)(2,1)S(1)}, u32[]{:S(2)}, u32[]{:S(2)}) collective-permute-start(bf16[1792,1,96]{0,2,1:T(8,128)(2,1)S(1)} %get-tuple-element.4), channel_id=1, source_target_pairs={{0,28},{4,24},{8,20},{12,16},{16,12},{20,8},{24,4},{28,0},{1,29},{... | collective-permute-start | bytes 1032200 | tf_op jit(solution)/shard_map/ppermute | solution.py:96
  666.1 63.9 %collective-permute-start.5 = (bf16[1792,1,96]{0,2,1:T(8,128)(2,1)S(1)}, bf16[1792,1,96]{0,2,1:T(8,128)(2,1)S(1)}, u32[]{:S(2)}, u32[]{:S(2)}) collective-permute-start(bf16[1792,1,96]{0,2,1:T(8,128)(2,1)S(1)} %get-tuple-element.5), channel_id=1, source_target_pairs={{0,24},{4,28},{8,16},{12,20},{16,8},{20,12},{24,0},{28,4},{1,25},{... | collective-permute-start | bytes 1032200 | tf_op jit(solution)/shard_map/ppermute | solution.py:96
  667.5 62.4 %collective-permute-start.4 = (bf16[1792,1,96]{0,2,1:T(8,128)(2,1)S(1)}, bf16[1792,1,96]{0,2,1:T(8,128)(2,1)S(1)}, u32[]{:S(2)}, u32[]{:S(2)}) collective-permute-start(bf16[1792,1,96]{0,2,1:T(8,128)(2,1)S(1)} %get-tuple-element.6), channel_id=1, source_target_pairs={{0,20},{4,16},{8,28},{12,24},{16,4},{20,0},{24,12},{28,8},{1,21},{... | collective-permute-start | bytes 1032200 | tf_op jit(solution)/shard_map/ppermute | solution.py:96
  669.0 31.5 %collective-permute-start.2 = (bf16[1792,1,96]{0,2,1:T(8,128)(2,1)S(1)}, bf16[1792,1,96]{0,2,1:T(8,128)(2,1)S(1)}, u32[]{:S(2)}, u32[]{:S(2)}) collective-permute-start(bf16[1792,1,96]{0,2,1:T(8,128)(2,1)S(1)} %get-tuple-element.8), channel_id=1, source_target_pairs={{0,12},{4,8},{8,4},{12,0},{16,28},{20,24},{24,20},{28,16},{1,13},{... | collective-permute-start | bytes 1032200 | tf_op jit(solution)/shard_map/ppermute | solution.py:96
  671.4 58.5 %collective-permute-start.3 = (bf16[1792,1,96]{0,2,1:T(8,128)(2,1)S(1)}, bf16[1792,1,96]{0,2,1:T(8,128)(2,1)S(1)}, u32[]{:S(2)}, u32[]{:S(2)}) collective-permute-start(bf16[1792,1,96]{0,2,1:T(8,128)(2,1)S(1)} %get-tuple-element.7), channel_id=1, source_target_pairs={{0,16},{4,20},{8,24},{12,28},{16,0},{20,4},{24,8},{28,12},{1,17},{... | collective-permute-start | bytes 1032200 | tf_op jit(solution)/shard_map/ppermute | solution.py:96
  730.1 4.6 copy-start.6
Sparse Core Ops, SparseCore 0:
  561.6 88.1 reduce-scatter.1
